TPU v7x, 256 devices: a whole 4x4x8 slice. The times are simulated.
256 devices in a mesh: tm: 32 (over x, z_hi, core), head: 8 (over z_lo, y).
Axes of the slice: x: 4, y: 4, z: 8 (z_hi: 4, z_lo: 2; z = z_hi * 2 + z_lo), core: 2. Of those that a mesh axis runs over, the one named last changes fastest.
Arguments:
- query_states: bfloat16 [49152, 1024], P('tm', 'head'), may hold values from -30 to 30
- key_states: bfloat16 [49152, 1024], P('tm', 'head'), may hold values from -30 to 30
- value_states: bfloat16 [49152, 1024], P('tm', 'head'), may hold values from -6 to 6
- win_start: int32 [64], P('tm'), may hold values from 0 to 62, as said below
- group_end: int32 [64], P('tm'), may hold values from 0 to 63, as said below
- out_weight: bfloat16 [1024, 1536], replicated, may hold values from -0.1875 to 0.1875
Outputs:
- projected: bfloat16 [49152, 1536], P(('tm', 'head'))
Inputs may be any that keep to these rules, and one draw needn't show every extreme that they name: For every frame f, win_start[f] = max(f - lag, 0) with a lag of 1 to 3; frame 64 - 2 has a lag of 3 in every draw, and the last frame has a lag of 1. `group_end`: frames 2p and 2p + 1 form one group (both end at 2p + 1) or two groups of one frame (each ends at itself); both kinds occur in every draw.
All inputs are finite; a program needn't handle non-finite values.
Results may differ from a plain program's by a relative error of at most 0.0051.
Values may be sent and summed in bfloat16 or wider, within the bound.
A program may use at most 64 MiB of HBM per device.

v0:
```python
import jax
import jax.numpy as jnp
from jax import lax
from jax.sharding import PartitionSpec as P

HD = 128
FT = 768


def spread(block, axis, owner):
    block = jnp.where(lax.axis_index(axis) == owner, block, jnp.zeros_like(block))
    return lax.psum(block, axis)


def from_behind(array, axis, by):
    length = lax.axis_size(axis)
    pairs = [(i, i + by) for i in range(length) if 0 <= i + by < length]
    return lax.ppermute(array, axis, pairs)


def attend(query_rows, key_rows, value_rows, visible):
    heads_here = query_rows.shape[1] // HD
    query_heads = query_rows.reshape(query_rows.shape[0], heads_here, HD)
    key_heads = key_rows.reshape(key_rows.shape[0], heads_here, HD)
    value_heads = value_rows.reshape(value_rows.shape[0], heads_here, HD)
    scores = jnp.einsum(
        "qhd,khd->hqk", query_heads, key_heads, preferred_element_type=jnp.float32
    ) * HD ** (-0.5)
    scores = jnp.where(visible[None, None, :], scores, -1e30)
    peak = jnp.max(scores, axis=-1, keepdims=True)
    weights = jnp.where(visible[None, None, :], jnp.exp(scores - peak), 0.0)
    total = jnp.sum(weights, axis=-1)
    rounded = weights.astype(jnp.bfloat16)
    mixed = jnp.einsum("hqk,khd->qhd", rounded, value_heads, preferred_element_type=jnp.float32)
    mixed = mixed / jnp.transpose(total)[:, :, None]
    return mixed.astype(jnp.bfloat16).reshape(query_rows.shape[0], query_rows.shape[1])


def local(query_states, key_states, value_states, win_start, group_end, out_weight):
    local_frames = win_start.shape[0]
    stacked = jnp.stack([key_states, value_states])
    sink_frame = stacked[:, :FT]
    sink_states = spread(sink_frame, "tm", 0)
    near_count = min(3, local_frames)
    far_count = 3 - near_count
    near_frames = from_behind(stacked, "tm", 1)
    pieces = []
    far_frames = from_behind(stacked[:, (local_frames - far_count) * FT :], "tm", 2)
    pieces.append(far_frames)
    extended = jnp.concatenate(pieces + [near_frames, stacked], axis=1)
    first_id = lax.axis_index("tm") * local_frames - 3
    outputs = []
    for slot in range(local_frames):
        span_frames = 5 if slot % 2 == 0 else 4
        window = extended[:, slot * FT : (slot + span_frames) * FT]
        key_rows = jnp.concatenate([sink_states[0], window[0]], axis=0)
        value_rows = jnp.concatenate([sink_states[1], window[1]], axis=0)
        frame_ids = first_id + slot + jnp.arange(span_frames * FT, dtype=jnp.int32) // FT
        window_seen = (
            (frame_ids >= 1) & (frame_ids >= win_start[slot]) & (frame_ids <= group_end[slot])
        )
        visible = jnp.concatenate([jnp.ones((FT,), dtype=bool), window_seen])
        query_rows = query_states[slot * FT : (slot + 1) * FT]
        outputs.append(attend(query_rows, key_rows, value_rows, visible))
    attended = jnp.concatenate(outputs, axis=0)
    token_rows = lax.all_to_all(attended, "head", split_axis=0, concat_axis=1, tiled=True)
    return jnp.dot(token_rows, out_weight, preferred_element_type=jnp.float32).astype(jnp.bfloat16)


def solution(mesh):
    in_specs = (P("tm", "head"), P("tm", "head"), P("tm", "head"), P("tm"), P("tm"), P())
    out_specs = P(("tm", "head"), None)
    return jax.shard_map(local, mesh=mesh, in_specs=in_specs, out_specs=out_specs, check_vma=False)
```

profile of v0, /device:TPU:8, one launch (start us, length us, event | category | flops | bytes accessed | tf_op | source)
XLA Modules:
  0.0 344.9 jit_solution(8197452554077602024)
XLA Ops:
  6.5 2.2 pad_maximum_fusion
  8.8 2.6 collective-permute-start.1
  11.4 2.2 fusion.58
  13.6 0.0 all-reduce.4.cloned.1.call-update
  13.6 5.2 %collective-permute-start = (bf16[2,768,128]{2,1,0:T(8,128)(2,1)}, bf16[2,768,128]{2,1,0:T(8,128)(2,1)}, u32[]{:S(2)}, u32[]{:S(2)}) collective-permute-start(bf16[2,768,128]{2,1,0:T(8,128)(2,1)} %get-tuple-element.9), channel_id=1, source_target_pairs={{0,16},{8,24},{16,32},{24,40},{32,48},{40,56},{48,64},{56,72},{64,... | collective-permute-start | bytes 1179656 | tf_op jit(solution)/shard_map/ppermute | solution.py:18
  18.8 1.3 fusion.81
  20.2 1.3 fusion.82
  21.4 1.1 compare_and_fusion.1
  22.6 1.2 compare_and_fusion
  23.8 275.4 %all-reduce.4.cloned.1.call-done = bf16[2,768,128]{2,1,0:T(8,128)(2,1)} async-done(((bf16[2,768,128]{2,1,0:T(8,128)(2,1)}), bf16[2,768,128]{2,1,0:T(8,128)(2,1)}) %all-reduce.4.cloned.1.call-update) | async-done | bytes 393232 | tf_op jit(solution)/shard_map/psum | solution.py:12
  299.2 1.1 slice_bitcast_fusion.5
  300.3 1.5 maximum_maximum_fusion.1
  301.8 0.1 slice_bitcast_fusion.3
  301.9 1.4 maximum_maximum_fusion
  303.3 0.1 slice_bitcast_fusion.1
  303.4 1.9 fusion.1
  305.4 3.9 %fusion.4 = f32[768]{0:T(1024)S(1)} fusion(f32[3840,768]{1,0:T(8,128)S(1)} %get-tuple-element.18, f32[768]{0:T(1024)S(1)} %get-tuple-element.17, pred[3840]{0:T(1024)(128)(4,1)S(1)} %concatenate.33), kind=kLoop, calls=%fused_computation.8 | loop fusion | flops 14744832 | bytes 11806464 | tf_op jit(solution)/shard_map/reduce_sum | solution.py:32
  309.3 2.3 fusion
  311.6 4.5 %fusion.2 = f32[768]{0:T(1024)S(1)} fusion(f32[4608,768]{1,0:T(8,128)S(1)} %get-tuple-element.20, f32[768]{0:T(1024)S(1)} %get-tuple-element.19, pred[4608]{0:T(1024)(128)(4,1)S(1)} %concatenate.29), kind=kLoop, calls=%fused_computation.6 | loop fusion | flops 17693952 | bytes 14166528 | tf_op jit(solution)/shard_map/reduce_sum | solution.py:32
  316.1 3.2 fusion.46
  319.4 3.8 %fusion.35 = bf16[768,128]{0,1:T(8,128)(2,1)S(1)} fusion(f32[4608,768]{1,0:T(8,128)S(1)} %get-tuple-element.20, f32[768]{0:T(1024)S(1)} %get-tuple-element.19, pred[4608]{0:T(1024)(128)(4,1)S(1)} %concatenate.29, bf16[3840,128]{1,0:T(8,128)(2,1)S(1)} %get-tuple-element.5, bf16[768,128]{1,0:T(8,128)(2,1)S(1)} %get-tuple-element.11, f32[768]{0:T(1024)S(1)} %fusion.2), kind=kOutput, calls=%fused_computation.28 | convolution fusion | flops 926220288 | bytes 15542784 | tf_op jit(solution)/shard_map/hqk,khd->qhd/dot_general | solution.py:34
  323.3 0.9 copy.7
  324.2 12.3 %all_to_all.19 = bf16[8,192,128]{2,1,0:T(8,128)(2,1)S(1)} all-to-all(bf16[8,192,128]{2,1,0:T(8,128)(2,1)} %bitcast.60), channel_id=1, replica_groups=mesh['tm'=32,'head'=8] {'head'}, dimensions={0} | all-to-all | bytes 786432 | tf_op jit(solution)/shard_map/all_to_all | solution.py:66
  336.5 1.6 convolution_convert_fusion
  (14 shorter events, 0.1 us)
Async XLA Ops:
  6.5 329.9 %copy-start = (bf16[1024,1536]{1,0:T(8,128)(2,1)S(1)}, bf16[1024,1536]{1,0:T(8,128)(2,1)}, u32[]{:S(2)}) copy-start(bf16[1024,1536]{1,0:T(8,128)(2,1)} %param.11) | copy-start | bytes 9437188
  6.5 295.4 %copy-start.1 = (bf16[1536,128]{1,0:T(8,128)(2,1)S(1)}, bf16[1536,128]{1,0:T(8,128)(2,1)}, u32[]{:S(2)}) copy-start(bf16[1536,128]{1,0:T(8,128)(2,1)} %param.8) | copy-start | bytes 1179652
  6.5 292.6 %all-reduce.4.cloned.1.call-start = ((), (), s32[]{:S(2)}) async-start(), calls=%async_computation.1 | async-start | bytes 786432 | tf_op jit(solution)/shard_map/psum | solution.py:12
  8.8 291.5 %collective-permute-start.1 = (bf16[2,1536,128]{2,1,0:T(8,128)(2,1)}, bf16[2,1536,128]{2,1,0:T(8,128)(2,1)}, u32[]{:S(2)}, u32[]{:S(2)}) collective-permute-start(bf16[2,1536,128]{2,1,0:T(8,128)(2,1)} %pad_maximum_fusion), channel_id=1, source_target_pairs={{0,8},{8,16},{16,24},{24,32},{32,40},{40,48},{48,56},{56,64},{64,7... | collective-permute-start | bytes 2359304 | tf_op jit(solution)/shard_map/ppermute | solution.py:18
  13.6 288.3 %collective-permute-start = (bf16[2,768,128]{2,1,0:T(8,128)(2,1)}, bf16[2,768,128]{2,1,0:T(8,128)(2,1)}, u32[]{:S(2)}, u32[]{:S(2)}) collective-permute-start(bf16[2,768,128]{2,1,0:T(8,128)(2,1)} %get-tuple-element.9), channel_id=1, source_target_pairs={{0,16},{8,24},{16,32},{24,40},{32,48},{40,56},{48,64},{56,72},{64,... | collective-permute-start | bytes 1179656 | tf_op jit(solution)/shard_map/ppermute | solution.py:18
  299.2 2.7 copy-start.2
  301.8 1.7 copy-start.3
Sparse Core Ops, SparseCore 0:
  13.7 285.4 all-reduce.3
where the time goes:
time: 345 us
  waiting for transfers between devices  275 us (80%)
  other arithmetic  18 us (5%)
  between operations  13.5 us (4%)
  matrix products  12.9 us (4%)
  blocking collectives  12.3 us (4%)
  starting transfers between devices  7.88 us (2%)
  local copies, waits for them, and re-layouts  4.87 us (1%)
    psum x1, waiting for transfers between devices, spread(): return lax.psum(block, axis)  275 us
    all_to_all x1, blocking collectives, local(): lax.all_to_all(attended, 'head', split_axis=0, concat_axis=1, tiled=True)  12.3 us
    reduce_sum x2, other arithmetic, attend(): total = jnp.sum(weights, axis=-1)  8.39 us
    ppermute x2, starting transfers between devices, from_behind(): return lax.ppermute(array, axis, pairs)  7.88 us
    dot_general x2, matrix products, attend(): jnp.einsum('hqk,khd->qhd', rounded, value_heads, preferred_element_type=j...  7.06 us
  transfers between devices with their start and end apart: 3, of which 1 were waited for; matrix products, arithmetic and copies ran while one was open for 3% of the time, Pallas kernels for 0%

commit v1 on v0

--- a/solution.py
+++ b/solution.py
@@ -7,9 +7,14 @@
 FT = 768
 
 
+def row_arrange(u_in, peer_axis):
+    work_now = jnp.sum(lax.all_gather(u_in, peer_axis), axis=0)
+    return work_now
+
+
 def spread(block, axis, owner):
     block = jnp.where(lax.axis_index(axis) == owner, block, jnp.zeros_like(block))
-    return lax.psum(block, axis)
+    return row_arrange(block, axis)
 
 
 def from_behind(array, axis, by):

time: 345 us -> 178 us (0.52)
  waiting for transfers between devices: 275 us -> 95.3 us
  other arithmetic: 18 us -> 25.2 us
    psum x1 -> x0, waiting for transfers between devices: 275 us -> none  [spread(): return lax.psum(block, axis)]
    all_gather x0 -> x1, waiting for transfers between devices: none -> 87.6 us  [row_arrange(): work_now = jnp.sum(lax.all_gather(u_in, peer_axis), axis=0)]
    ppermute x2, waiting for transfers between devices: 0.01 us -> 7.75 us  [from_behind(): return lax.ppermute(array, axis, pairs)]
    reduce_sum x0 -> x1, other arithmetic: none -> 6.72 us  [row_arrange(): work_now = jnp.sum(lax.all_gather(u_in, peer_axis), axis=0)]
  transfers between devices with their start and end apart: 3 -> 3, of which waited for: 1 -> 2; matrix products, arithmetic and copies ran while one was open for 3% -> 7% of each run, Pallas kernels for 0% -> 0%
where the time goes in v1:
time: 178 us; the launch traced here: 176 us
  waiting for transfers between devices  95.3 us (54%)
  other arithmetic  25.2 us (14%)
  matrix products  15.5 us (9%)
  between operations  13.6 us (8%)
  blocking collectives  12.5 us (7%)
  starting transfers between devices  7.86 us (4%)
  local copies, waits for them, and re-layouts  6.4 us (4%)
    all_gather x1, waiting for transfers between devices, row_arrange(): work_now = jnp.sum(lax.all_gather(u_in, peer_axis), axis=0)  87.6 us
    all_to_all x1, blocking collectives, local(): lax.all_to_all(attended, 'head', split_axis=0, concat_axis=1, tiled=True)  12.5 us
    reduce_sum x2, other arithmetic, attend(): total = jnp.sum(weights, axis=-1)  8.4 us
    ppermute x2, starting transfers between devices, from_behind(): return lax.ppermute(array, axis, pairs)  7.85 us
    ppermute x2, waiting for transfers between devices, from_behind(): return lax.ppermute(array, axis, pairs)  7.75 us
    dot_general x2, matrix products, attend(): jnp.einsum('qhd,khd->hqk', query_heads, key_heads, preferred_element_type...  7.14 us
    dot_general x2, matrix products, attend(): jnp.einsum('hqk,khd->qhd', rounded, value_heads, preferred_element_type=j...  6.78 us
    reduce_sum x1, other arithmetic, row_arrange(): work_now = jnp.sum(lax.all_gather(u_in, peer_axis), axis=0)  6.72 us
  transfers between devices with their start and end apart: 3, of which 2 were waited for; matrix products, arithmetic and copies ran while one was open for 7% of the time, Pallas kernels for 0%

profile of v1, /device:TPU:8, one launch (start us, length us, event | category | flops | bytes accessed | tf_op | source)
XLA Modules:
  0.0 176.4 jit_solution(18057666262837697530)
XLA Ops:
  6.5 2.3 %fusion.58 = (bf16[2,768,128]{2,1,0:T(8,128)(2,1)}, bf16[2,768,128]{2,1,0:T(8,128)(2,1)}) fusion(bf16[1,1536,128]{2,1,0:T(8,128)(2,1)} %bitcast.58, bf16[1,1536,128]{2,1,0:T(8,128)(2,1)} %bitcast.54, pred[]{:T(512)S(6)} %eq.3), kind=kLoop, calls=%fused_computation.50 | loop fusion | flops 589824 | bytes 1572865 | tf_op jit(solution)/shard_map/stack | solution.py:46
  8.9 2.1 %pad_maximum_fusion = bf16[2,1536,128]{2,1,0:T(8,128)(2,1)} fusion(bf16[1,1536,128]{2,1,0:T(8,128)(2,1)} %bitcast.55, bf16[1,1536,128]{2,1,0:T(8,128)(2,1)} %bitcast.59), kind=kLoop, calls=%fused_computation.34 | loop fusion | flops 393216 | bytes 1572864 | tf_op jit(solution)/shard_map/stack | solution.py:46
  11.0 2.6 %collective-permute-start.1 = (bf16[2,1536,128]{2,1,0:T(8,128)(2,1)}, bf16[2,1536,128]{2,1,0:T(8,128)(2,1)}, u32[]{:S(2)}, u32[]{:S(2)}) collective-permute-start(bf16[2,1536,128]{2,1,0:T(8,128)(2,1)} %pad_maximum_fusion), channel_id=1, source_target_pairs={{0,8},{8,16},{16,24},{24,32},{32,40},{40,48},{48,56},{56,64},{64,7... | collective-permute-start | bytes 2359304 | tf_op jit(solution)/shard_map/ppermute | solution.py:23
  13.6 5.2 %collective-permute-start = (bf16[2,768,128]{2,1,0:T(8,128)(2,1)}, bf16[2,768,128]{2,1,0:T(8,128)(2,1)}, u32[]{:S(2)}, u32[]{:S(2)}) collective-permute-start(bf16[2,768,128]{2,1,0:T(8,128)(2,1)} %get-tuple-element.9), channel_id=1, source_target_pairs={{0,16},{8,24},{16,32},{24,40},{32,48},{40,56},{48,64},{56,72},{64,... | collective-permute-start | bytes 1179656 | tf_op jit(solution)/shard_map/ppermute | solution.py:23
  18.9 1.4 fusion.81
  20.3 1.3 fusion.82
  21.6 1.3 compare_and_fusion
  22.9 1.3 compare_and_fusion.1
  24.2 1.6 maximum_maximum_fusion.1
  25.7 7.7 %collective-permute-done = bf16[2,768,128]{2,1,0:T(8,128)(2,1)} collective-permute-done((bf16[2,768,128]{2,1,0:T(8,128)(2,1)}, bf16[2,768,128]{2,1,0:T(8,128)(2,1)}, u32[]{:S(2)}, u32[]{:S(2)}) %collective-permute-start) | collective-permute-done | bytes 393248 | tf_op jit(solution)/shard_map/ppermute | solution.py:23
  33.5 1.5 maximum_maximum_fusion
  35.0 1.3 slice_bitcast_fusion.3
  36.3 1.4 slice_bitcast_fusion.1
  37.7 87.6 %all-gather.3.cloned.1.call-done = bf16[64,768,128]{2,1,0:T(8,128)(2,1)} async-done(((bf16[2,768,128]{2,1,0:T(8,128)(2,1)}), bf16[64,768,128]{2,1,0:T(8,128)(2,1)}) %all-gather.3.cloned.1.call-update) | async-done | bytes 12582928 | tf_op jit(solution)/shard_map/all_gather | solution.py:11
  125.3 6.7 %reduce_sum.30 = bf16[2,768,128]{2,1,0:T(8,128)(2,1)S(1)} reduce(bf16[32,2,768,128]{3,2,1,0:T(8,128)(2,1)} %bitcast.53, bf16[]{:T(256)} %constant.12.clone.1), dimensions={0}, to_apply=%region_0.1 | reduce | flops 6094848 | bytes 12976130 | tf_op jit(solution)/shard_map/reduce_sum | solution.py:11
  132.0 4.8 %fusion.1 = (f32[768]{0:T(1024)S(1)}, f32[3840,768]{1,0:T(8,128)S(1)}) fusion(pred[3840]{0:T(1024)(128)(4,1)S(1)} %concatenate.33, bf16[1536,128]{1,0:T(8,128)(2,1)} %param.6, bf16[3072,128]{1,0:T(8,128)(2,1)} %get-tuple-element.8, bf16[768,128]{1,0:T(8,128)(2,1)S(1)} %get-tuple-element.12), kind=kOutput, calls=%fused_computation.5 | convolution fusion | flops 765787392 | bytes 12983040 | tf_op jit(solution)/shard_map/qhd,khd->hqk/dot_general | solution.py:31
  136.9 3.7 %fusion.4 = f32[768]{0:T(1024)S(1)} fusion(f32[3840,768]{1,0:T(8,128)S(1)} %get-tuple-element.18, f32[768]{0:T(1024)S(1)} %get-tuple-element.17, pred[3840]{0:T(1024)(128)(4,1)S(1)} %concatenate.33), kind=kLoop, calls=%fused_computation.8 | loop fusion | flops 14744832 | bytes 11806464 | tf_op jit(solution)/shard_map/reduce_sum | solution.py:37
  140.6 2.3 %fusion = (f32[768]{0:T(1024)S(1)}, f32[4608,768]{1,0:T(8,128)S(1)}) fusion(pred[4608]{0:T(1024)(128)(4,1)S(1)} %concatenate.29, bf16[1536,128]{1,0:T(8,128)(2,1)S(1)} %copy-done.5, bf16[3840,128]{1,0:T(8,128)(2,1)S(1)} %copy-done.3, bf16[768,128]{1,0:T(8,128)(2,1)S(1)} %get-tuple-element.12), kind=kOutput, calls=%fused_computation.2 | convolution fusion | flops 918945024 | bytes 15540224 | tf_op jit(solution)/shard_map/qhd,khd->hqk/dot_general | solution.py:31
  142.9 4.7 %fusion.2 = f32[768]{0:T(1024)S(1)} fusion(f32[4608,768]{1,0:T(8,128)S(1)} %get-tuple-element.20, f32[768]{0:T(1024)S(1)} %get-tuple-element.19, pred[4608]{0:T(1024)(128)(4,1)S(1)} %concatenate.29), kind=kLoop, calls=%fused_computation.6 | loop fusion | flops 17693952 | bytes 14166528 | tf_op jit(solution)/shard_map/reduce_sum | solution.py:37
  147.7 3.1 %fusion.46 = bf16[768,128]{0,1:T(8,128)(2,1)S(1)} fusion(f32[3840,768]{1,0:T(8,128)S(1)} %get-tuple-element.18, f32[768]{0:T(1024)S(1)} %get-tuple-element.17, pred[3840]{0:T(1024)(128)(4,1)S(1)} %concatenate.33, bf16[3072,128]{1,0:T(8,128)(2,1)S(1)} %copy-done.4, bf16[768,128]{1,0:T(8,128)(2,1)S(1)} %get-tuple-element.11, f32[768]{0:T(1024)S(1)} %fusion.4), kind=kOutput, calls=%fused_computation.31 | convolution fusion | flops 771883008 | bytes 12986112 | tf_op jit(solution)/shard_map/hqk,khd->qhd/dot_general | solution.py:39
  150.8 3.7 %fusion.35 = bf16[768,128]{0,1:T(8,128)(2,1)S(1)} fusion(f32[4608,768]{1,0:T(8,128)S(1)} %get-tuple-element.20, f32[768]{0:T(1024)S(1)} %get-tuple-element.19, pred[4608]{0:T(1024)(128)(4,1)S(1)} %concatenate.29, bf16[3840,128]{1,0:T(8,128)(2,1)S(1)} %copy-done.2, bf16[768,128]{1,0:T(8,128)(2,1)S(1)} %get-tuple-element.11, f32[768]{0:T(1024)S(1)} %fusion.2), kind=kOutput, calls=%fused_computation.28 | convolution fusion | flops 926220288 | bytes 15542784 | tf_op jit(solution)/shard_map/hqk,khd->qhd/dot_general | solution.py:39
  154.5 0.9 copy.9
  155.4 12.5 %all_to_all.19 = bf16[8,192,128]{2,1,0:T(8,128)(2,1)S(1)} all-to-all(bf16[8,192,128]{2,1,0:T(8,128)(2,1)} %bitcast.62), channel_id=1, replica_groups=mesh['tm'=32,'head'=8] {'head'}, dimensions={0} | all-to-all | bytes 786432 | tf_op jit(solution)/shard_map/all_to_all | solution.py:71
  167.9 1.6 convolution_convert_fusion
  (19 shorter events, 0.1 us)
Async XLA Ops:
  6.5 161.4 %copy-start = (bf16[1024,1536]{1,0:T(8,128)(2,1)S(1)}, bf16[1024,1536]{1,0:T(8,128)(2,1)}, u32[]{:S(2)}) copy-start(bf16[1024,1536]{1,0:T(8,128)(2,1)} %param.11) | copy-start | bytes 9437188
  6.5 26.9 %copy-start.1 = (bf16[1536,128]{1,0:T(8,128)(2,1)S(1)}, bf16[1536,128]{1,0:T(8,128)(2,1)}, u32[]{:S(2)}) copy-start(bf16[1536,128]{1,0:T(8,128)(2,1)} %param.8) | copy-start | bytes 1179652
  6.5 118.7 %all-gather.3.cloned.1.call-start = ((), (), s32[]{:S(2)}) async-start(), calls=%async_computation.1 | async-start | bytes 12976128 | tf_op jit(solution)/shard_map/all_gather | solution.py:11
  11.0 13.2 %collective-permute-start.1 = (bf16[2,1536,128]{2,1,0:T(8,128)(2,1)}, bf16[2,1536,128]{2,1,0:T(8,128)(2,1)}, u32[]{:S(2)}, u32[]{:S(2)}) collective-permute-start(bf16[2,1536,128]{2,1,0:T(8,128)(2,1)} %pad_maximum_fusion), channel_id=1, source_target_pairs={{0,8},{8,16},{16,24},{24,32},{32,40},{40,48},{48,56},{56,64},{64,7... | collective-permute-start | bytes 2359304 | tf_op jit(solution)/shard_map/ppermute | solution.py:23
  13.6 19.8 %collective-permute-start = (bf16[2,768,128]{2,1,0:T(8,128)(2,1)}, bf16[2,768,128]{2,1,0:T(8,128)(2,1)}, u32[]{:S(2)}, u32[]{:S(2)}) collective-permute-start(bf16[2,768,128]{2,1,0:T(8,128)(2,1)} %get-tuple-element.9), channel_id=1, source_target_pairs={{0,16},{8,24},{16,32},{24,40},{32,48},{40,56},{48,64},{56,72},{64,... | collective-permute-start | bytes 1179656 | tf_op jit(solution)/shard_map/ppermute | solution.py:23
  136.8 3.7 %copy-start.3 = (bf16[3840,128]{1,0:T(8,128)(2,1)S(1)}, bf16[3840,128]{1,0:T(8,128)(2,1)}, u32[]{:S(2)}) copy-start(bf16[3840,128]{1,0:T(8,128)(2,1)} %get-tuple-element.6) | copy-start | bytes 2949124
  136.9 3.7 %copy-start.5 = (bf16[1536,128]{1,0:T(8,128)(2,1)S(1)}, bf16[1536,128]{1,0:T(8,128)(2,1)}, u32[]{:S(2)}) copy-start(bf16[1536,128]{1,0:T(8,128)(2,1)} %param.6) | copy-start | bytes 1179652
  142.9 4.7 %copy-start.4 = (bf16[3072,128]{1,0:T(8,128)(2,1)S(1)}, bf16[3072,128]{1,0:T(8,128)(2,1)}, u32[]{:S(2)}) copy-start(bf16[3072,128]{1,0:T(8,128)(2,1)} %get-tuple-element.7) | copy-start | bytes 2359300
  147.6 3.1 %copy-start.2 = (bf16[3840,128]{1,0:T(8,128)(2,1)S(1)}, bf16[3840,128]{1,0:T(8,128)(2,1)}, u32[]{:S(2)}) copy-start(bf16[3840,128]{1,0:T(8,128)(2,1)} %get-tuple-element.5) | copy-start | bytes 2949124
Sparse Core Ops, SparseCore 0:
  9.9 115.3 all-gather.2
